TPU v7x, 32 devices: a whole 2x2x4 slice. The times are simulated.
32 devices in a mesh: groups: 2 (over x), context: 16 (over z, y, core).
Axes of the slice: x: 2, y: 2, z: 4, core: 2. Of those that a mesh axis runs over, the one named last changes fastest.
Arguments:
- query_rows: bfloat16 [8192, 1536], P(('groups', 'context')), parts along dimension 0, may hold values from -9 to 9
- key_rows: bfloat16 [8192, 1536], P(('groups', 'context')), parts along dimension 0, may hold values from -9 to 9
- value_rows: bfloat16 [8192, 1536], P(('groups', 'context')), parts along dimension 0, may hold values from -6 to 6
- extents: int32 [12, 3], replicated, may hold values from 1 to 3, as said below
Outputs:
- attended: bfloat16 [8192, 1536], P(('groups', 'context')), parts along dimension 0
There are 2 independent parts, one for each index of `groups`. A program takes and returns all parts, laid end to end along the dimension named above; an argument that names none is the same for every part. Nothing has to cross between parts.
Inputs may be any that keep to these rules, and one draw needn't show every extreme that they name: Every entry is 1 or 3; some head has extents 3, 3, 3.
All inputs are finite; a program needn't handle non-finite values.
Results may differ from a plain program's by a relative error of at most 0.004.
Values may be sent and summed in bfloat16 or wider, within the bound.
No kernel may reach another device: no remote copies, remote signals or barrier semaphores. Data moves between devices by JAX's collectives and lax.ppermute only.
A program may use at most 64 MiB of HBM per device.

v0:
```python
import functools
import math

import jax
import jax.numpy as jnp
from jax import lax
from jax.experimental import pallas as pl
from jax.experimental.pallas import tpu as pltpu
from jax.sharding import PartitionSpec as P

HEADS = 12
HD = 128
HT = 8
ROWS = 256
MASKED = -1e30
SCALE2 = math.log2(math.e) / math.sqrt(HD)
PACK_LIMIT = 62
FILL_EARLY, FILL, WAIT = 2e10, 8e9, 8e9
MENU = ((2, 2, 3), (3, 2, 3), (3, 2, 4), (4, 2, 3), (4, 2, 4), (5, 2, 4), (6, 2, 3), (7, 2, 2), (9, 1, 1), (12, 0, 0))

TALL, WIDE, TIMED, UP_OK, DOWN_OK, SIDE_OK = 12, 24, 36, 48, 49, 50
SCHEDULE = 64
ANY = pl.BlockSpec(memory_space=pl.ANY)
VMEM = pl.BlockSpec(memory_space=pltpu.VMEM)
SMEM = pl.BlockSpec(memory_space=pltpu.SMEM)


def plan_kernel(time_tiles, extents, index, schedule, chosen):
    one, none = jnp.int32(1), jnp.int32(0)
    wide, timed, tall = [], [], []
    for head in range(HEADS):
        wide.append(jnp.where((extents[2, head] - 1) // 2 >= 0, one, none))
        timed.append(jnp.where((extents[0, head] - 1) // 2 >= 1, one, none))
        tall.append(jnp.where((extents[1, head] - 1) // 2 >= 1, one, none))
    both = sum(t * h for t, h in zip(timed, tall))
    only_timed = sum(timed) - both
    only_tall = sum(tall) - both
    choice, a, b, c = (jnp.int32(x) for x in (len(MENU) - 1, *MENU[-1]))
    for place in reversed(range(len(MENU) - 1)):
        sizes = MENU[place]
        fits = both + jnp.maximum(only_timed - sizes[1], 0) + jnp.maximum(only_tall - sizes[2], 0) <= sizes[0]
        choice, a, b, c = (jnp.where(fits, jnp.int32(x), y) for x, y in zip((place, *sizes), (choice, a, b, c)))
    timed_in_a = jnp.maximum(only_timed - b, 0)
    tall_in_a = jnp.maximum(only_tall - c, 0)
    end_a = both + timed_in_a + tall_in_a
    end_b = a + only_timed - timed_in_a
    end_c = a + b + only_tall - tall_in_a
    seen = [none] * 4
    for head in range(HEADS):
        t, h = timed[head] == 1, tall[head] == 1
        rank = jnp.where(t, jnp.where(h, seen[0], seen[1]), jnp.where(h, seen[2], seen[3]))
        from_timed = jnp.where(rank < timed_in_a, both + rank, a + rank - timed_in_a)
        from_tall = jnp.where(rank < tall_in_a, both + timed_in_a + rank, a + b + rank - tall_in_a)
        left = rank - (a - end_a)
        later = left - (a + b - end_b)
        last = later - (a + b + c - end_c)
        free = jnp.where(
            left < 0, end_a + rank, jnp.where(later < 0, end_b + left, jnp.where(last < 0, end_c + later, a + b + c + last))
        )
        place = jnp.where(t, jnp.where(h, rank, from_timed), jnp.where(h, from_tall, free))
        for kind, is_kind in enumerate((t & h, t & ~h, ~t & h, ~t & ~h)):
            seen[kind] = seen[kind] + jnp.where(is_kind, one, none)
        schedule[place] = jnp.int32(head)
        schedule[TALL + place] = tall[head]
        schedule[WIDE + place] = wide[head]
        schedule[TIMED + place] = timed[head]
    time_index, height_index = lax.div(index[0], jnp.int32(HT)), lax.rem(index[0], jnp.int32(HT))
    schedule[UP_OK] = jnp.where(height_index > 0, one, none)
    schedule[DOWN_OK] = jnp.where(height_index < HT - 1, one, none)
    schedule[SIDE_OK] = jnp.where(time_index > 0, one, none)
    schedule[SIDE_OK + 1] = jnp.where(time_index < time_tiles - 1, one, none)
    chosen[0] = choice
    for place in range(SIDE_OK + 2, SCHEDULE):
        schedule[place] = none


def plan(extents, index, time_tiles):
    return pl.pallas_call(
        functools.partial(plan_kernel, time_tiles),
        out_shape=[jax.ShapeDtypeStruct((SCHEDULE,), jnp.int32), jax.ShapeDtypeStruct((1,), jnp.int32)],
        in_specs=[SMEM, SMEM],
        out_specs=[SMEM, SMEM],
        name="plan",
    )(extents.T, index)


def each(count, body):
    def one(place, carry):
        body(place)
        return carry

    if count > 1:
        lax.fori_loop(0, count, one, 0)
    elif count:
        body(0)


def levels_of(a):
    return -(-a // 8) * 8


def columns(schedule, place):
    return pl.ds(pl.multiple_of(schedule[place] * HD, HD), HD)


def call(kernel, schedule, operands, outs, scratch=(), specs=None, out_specs=None, aliases=None, cost=None, name=None, limit=40):
    return pl.pallas_call(
        kernel,
        out_shape=outs,
        grid_spec=pltpu.PrefetchScalarGridSpec(
            num_scalar_prefetch=1,
            in_specs=specs or [VMEM] * len(operands),
            out_specs=out_specs or [VMEM] * len(outs),
            scratch_shapes=list(scratch),
        ),
        input_output_aliases=aliases or {},
        compiler_params=pltpu.CompilerParams(vmem_limit_bytes=limit * 2**20),
        cost_estimate=cost,
        name=name,
    )(schedule, *operands)


LONG = pl.CostEstimate(flops=10**11, bytes_accessed=10**6, transcendentals=0)
SHORT = pl.CostEstimate(flops=10**6, bytes_accessed=10**5, transcendentals=0)


def hint(flops):
    return pl.CostEstimate(flops=int(flops), bytes_accessed=10**5, transcendentals=0)


def pack_kernel(firsts, sources, apart, schedule, *refs):
    inputs, outs, sems = refs[:sources], list(refs[sources:-1]), refs[-1]
    if apart:
        outs[:sources] = [outs[:sources]]

    def copies(act):
        for first, out in zip(firsts, outs):
            for which, source in enumerate(inputs):
                target = out[which] if isinstance(out, list) else out.at[which]

                def one(place):
                    at = columns(schedule, first + place)
                    act(pltpu.make_async_copy(source.at[:, at], target.at[place], sems.at[first + place, which]))

                each(target.shape[0], one)

    copies(lambda copy: copy.start())
    copies(lambda copy: copy.wait())


def pack(schedule, sources, pieces, apart, limit=40):
    pieces = [(first, size) for first, size in pieces if size]
    shapes = [(len(sources), size, ROWS, HD) for _, size in pieces]
    if apart:
        shapes[:1] = [shapes[0][1:]] * len(sources)
    return list(call(
        functools.partial(pack_kernel, [first for first, _ in pieces], len(sources), apart),
        schedule,
        sources,
        [jax.ShapeDtypeStruct(shape, sources[0].dtype) for shape in shapes],
        scratch=[pltpu.SemaphoreType.DMA((HEADS, len(sources)))],
        specs=[ANY] * len(sources),
        cost=SHORT,
        name="pack",
        limit=limit,
    ))


def attend(query, slabs):
    scores, tops = [], []
    for key, _, ok in slabs:
        score = lax.dot_general(key, query, (((1,), (1,)), ((), ())), preferred_element_type=jnp.float32)
        scores.append(score)
        tops.append(jnp.where(ok, jnp.max(score, axis=0, keepdims=True), jnp.float32(MASKED)))
    top = functools.reduce(jnp.maximum, tops)
    total, mixture = None, None
    for score, (_, value, ok) in zip(scores, slabs):
        weight = jnp.exp2((score - jnp.where(ok, top, jnp.float32(-MASKED))) * SCALE2)
        part = jnp.sum(weight, axis=0, keepdims=True)
        mixed = lax.dot_general(
            value, weight.astype(jnp.bfloat16), (((0,), (0,)), ((), ())), preferred_element_type=jnp.float32
        )
        total = part if total is None else total + part
        mixture = mixed if mixture is None else mixture + mixed
    return mixture * (1.0 / total), top * SCALE2 + jnp.log2(total)


def own_slab(schedule, place, k, v):
    at = columns(schedule, place)
    return k[:, at], v[:, at], schedule[WIDE + place] == 1


def tall_slabs(schedule, place, slot, heights):
    tall = schedule[TALL + place]
    if len(heights) == 2:
        heights = [piece.at[which] for piece in heights for which in range(2)]
    return [
        (heights[0][slot], heights[1][slot], tall * schedule[UP_OK] == 1),
        (heights[2][slot], heights[3][slot], tall * schedule[DOWN_OK] == 1),
    ]


def partial_kernel(schedule, q, k, v, *refs):
    heights, (out, levels) = refs[:-2], refs[-2:]
    a = q.shape[0]
    rows = levels.shape[0]
    levels[...] = jnp.zeros_like(levels)

    def body(place):
        slabs = [own_slab(schedule, place, k, v)] + tall_slabs(schedule, place, place, heights)
        mixture, level = attend(q[place], slabs)
        out[pl.ds(pl.multiple_of(place * HD, HD), HD), :] = mixture.astype(out.dtype)
        levels[pl.ds(place, 1), :] = level

    each(a, body)
    level = levels[...]
    pieces = []
    for _ in range(3):
        piece = level.astype(jnp.bfloat16)
        level = level - piece.astype(jnp.float32)
        pieces.append(piece)
    for place, piece in enumerate(pieces):
        out[pl.ds(a * HD + place * rows, rows), :] = piece


def partial_attention(schedule, q, k, v, heights):
    a = q.shape[0]
    return call(
        partial_kernel,
        schedule,
        [q, k, v, *heights],
        [jax.ShapeDtypeStruct((a * HD + 3 * levels_of(a), ROWS), jnp.bfloat16)],
        scratch=[pltpu.VMEM((levels_of(a), ROWS), jnp.float32)],
        cost=SHORT,
        name="partial_attention",
    )[0]


def local_kernel(schedule, q, k, v, *refs):
    heights, (mix, stat) = refs[:-2], refs[-2:]

    def body(place):
        slabs = [own_slab(schedule, place, k, v)] + tall_slabs(schedule, place, place, heights)
        mixture, level = attend(q[:, columns(schedule, place)], slabs)
        mix[place] = mixture
        stat[pl.ds(place, 1), :] = level

    each(mix.shape[0], body)


def local_attention(schedule, q, k, v, heights, a):
    return call(
        local_kernel,
        schedule,
        [q, k, v, *heights],
        [
            jax.ShapeDtypeStruct((a, HD, ROWS), jnp.float32),
            jax.ShapeDtypeStruct((levels_of(a), ROWS), jnp.float32),
        ],
        cost=SHORT,
        name="local_attention",
    )


def alone_kernel(first, schedule, q, k, v, out, result, sems):
    def body(slot):
        place = first + slot
        return attend(q[:, columns(schedule, place)], [own_slab(schedule, place, k, v)])[0].T

    store_columns(schedule, first, result.shape[0], out, result, sems, body)


def store_columns(schedule, first, count, out, result, sems, body):
    def one(slot):
        result[slot] = body(slot).astype(result.dtype)
        pltpu.make_async_copy(result.at[slot], out.at[:, columns(schedule, first + slot)], sems.at[slot]).start()

    def done(slot):
        pltpu.make_async_copy(result.at[slot], out.at[:, columns(schedule, first + slot)], sems.at[slot]).wait()

    each(count, one)
    each(count, done)


def side_ok(schedule, place, side):
    timed = schedule[TIMED + place]
    return (timed if side is None else timed * schedule[SIDE_OK + side]) == 1


def timed_kernel(a, sides, schedule, q, k, v, *refs):
    parts = refs[: len(sides)]
    out, result, sems = refs[-3:]

    def body(slot):
        place = a + slot
        slabs = [own_slab(schedule, place, k, v)]
        for side, part in zip(sides, parts):
            slabs.append((part[0, slot], part[1, slot], side_ok(schedule, place, side)))
        return attend(q[:, columns(schedule, place)], slabs)[0].T

    store_columns(schedule, a, result.shape[0], out, result, sems, body)


def tall_kernel(first, schedule, q, k, v, up, down, *refs):
    out, result, sems = refs[-3:]

    def body(slot):
        place = first + slot
        slabs = [own_slab(schedule, place, k, v)] + tall_slabs(schedule, place, slot, [up, down])
        return attend(q[:, columns(schedule, place)], slabs)[0].T

    store_columns(schedule, first, result.shape[0], out, result, sems, body)


def combine_kernel(sides, schedule, mix, stat, *refs):
    parts = refs[: len(sides)]
    out, result, sems, levels = refs[-4:]
    a, rows = mix.shape[0], stat.shape[0]
    for which, part in enumerate(parts):
        levels[which] = sum(part[pl.ds(a * HD + place * rows, rows), :].astype(jnp.float32) for place in range(3))

    def body(slot):
        every, mixtures = [stat[pl.ds(slot, 1), :]], [mix[slot]]
        for which, (side, part) in enumerate(zip(sides, parts)):
            level = levels[which, pl.ds(slot, 1), :]
            every.append(jnp.where(side_ok(schedule, slot, side), level, jnp.float32(MASKED)))
            mixtures.append(part[pl.ds(pl.multiple_of(slot * HD, HD), HD), :].astype(jnp.float32))
        top = functools.reduce(jnp.maximum, every)
        shares = [jnp.exp2(level - top) for level in every]
        inverse = 1.0 / functools.reduce(jnp.add, shares)
        return functools.reduce(jnp.add, [(share * inverse) * mixture for share, mixture in zip(shares, mixtures)]).T

    store_columns(schedule, 0, a, out, result, sems, body)


def into_columns(kernel, schedule, operands, out, count, scratch, cost, name):
    operands, aliases = (operands, {}) if out is None else ([*operands, out], {1 + len(operands): 0})
    return call(
        kernel,
        schedule,
        operands,
        [jax.ShapeDtypeStruct((ROWS, HEADS * HD), jnp.bfloat16)],
        scratch=[pltpu.VMEM((count, ROWS, HD), jnp.bfloat16), pltpu.SemaphoreType.DMA((count,)), *scratch],
        specs=[VMEM] * (len(operands) - len(aliases)) + [ANY] * len(aliases),
        out_specs=[ANY],
        aliases=aliases,
        cost=cost,
        name=name,
    )[0]


def after(value, *earlier):
    return lax.optimization_barrier((value, *earlier))[0]


def branch(a, b, c, time_tiles, q, k, v, schedule):
    count = time_tiles * HT
    if time_tiles == 2:
        routes = [[(i, (i + HT) % count) for i in range(count)]]
        sides = [None]
    else:
        routes = [[(i, i + HT) for i in range(count - HT)], [(i + HT, i) for i in range(count - HT)]]
        sides = [0, 1]
    backs = [[(there, here) for here, there in route] for route in routes]
    upward = [(i, i + 1) for i in range(count - 1) if i % HT != HT - 1]
    downward = [(there, here) for here, there in upward]

    def move(value, pairs):
        return lax.ppermute(value, "context", pairs)

    d = HEADS - a - b - c
    apart = a >= 2 * b and not d
    (queries,) = pack(schedule, [q], [(0, a)], True, PACK_LIMIT)
    sent = [move(queries, route) for route in routes]
    pieces = pack(schedule, after([k, v], queries), [(0, a), (a, b), (a + b, c)], apart)
    nears = [pieces.pop(0) for _ in range(2 if apart else 1)]
    across = pieces.pop(0) if b else None
    later = pieces.pop(0) if c else None
    near = [move(piece, pairs) for pairs in (upward, downward) for piece in nears]
    early = a > 3
    out, ready = None, schedule
    if d:
        kernel = functools.partial(alone_kernel, a + b + c)
        first = after(schedule, *(nears if early else sent))
        out = into_columns(kernel, first, [q, k, v], None, d, [], hint(FILL_EARLY if early else FILL), "alone")
        ready = schedule if early else after(schedule, out)
    if b:
        across = after(across, *(sent if a == 5 else []), *([out] if d and early else sent))
        others = [move(across, pairs) for pairs in routes]
    parts = [partial_attention(ready, query, k, v, near) for query in sent]
    if c:
        later = after(later, *(sent if a == 5 else []), *([out] if d else sent))
        heights = [move(later, upward), move(later, downward)]
    mix, stat = local_attention(after(schedule, *parts), q, k, v, near, a)
    parts = [move(part, back) for part, back in zip(parts, backs)]
    if b:
        kernel = functools.partial(timed_kernel, a, sides)
        out = into_columns(kernel, after(schedule, stat), [q, k, v, *others], out, b, [], hint(WAIT if a < 6 else 0), "timed")
    if c:
        kernel = functools.partial(tall_kernel, a + b)
        out = into_columns(kernel, after(schedule, stat), [q, k, v, *heights], out, c, [], LONG, "tall")
    scratch = [pltpu.VMEM((len(sides), levels_of(a), ROWS), jnp.float32)]
    return into_columns(
        functools.partial(combine_kernel, sides[::-1]), schedule, [mix, stat, *parts], out, a, scratch, LONG, "combine"
    )


def local(query_rows, key_rows, value_rows, extents):
    time_tiles = lax.axis_size("context") // HT
    index = lax.axis_index("context").astype(jnp.int32).reshape(1)
    schedule, choice = plan(extents, index, time_tiles)
    branches = [functools.partial(branch, *sizes, time_tiles) for sizes in MENU]
    return lax.switch(choice.reshape(()), branches, query_rows, key_rows, value_rows, schedule)


def solution(mesh):
    placed = P(("groups", "context"), None)
    return jax.shard_map(local, mesh=mesh, in_specs=(placed, placed, placed, P()), out_specs=placed, check_vma=False)
```

profile of v0, /device:TPU:1, one launch (start us, length us, event | category | flops | bytes accessed | tf_op | source)
XLA Modules:
  0.0 60.1 jit_solution(10951499351774030348)
XLA Ops:
  0.0 1.8 %plan.1 = (s32[64]{0:T(128)S(1)}, s32[1]{0:T(128)}) custom-call(s32[3,12]{1,0:T(4,128)} %bitcast.3, s32[1]{0:T(128)} %bitcast.1.index), custom_call_target="tpu_custom_call" | custom-call | tf_op jit(solution)/shard_map/plan/pallas_call | solution.py:78
  2.4 57.5 %conditional.1 = (bf16[256,1536]{1,0:T(8,128)(2,1)}) conditional(s32[]{:T(128)} %bitcast.2, (s32[64]{0:T(128)S(1)}, bf16[256,1536]{1,0:T(8,128)(2,1)}, bf16[256,1536]{1,0:T(8,128)(2,1)}, bf16[256,1536]{1,0:T(8,128)(2,1)}) %tuple.94, (s32[64]{0:T(128)S(1)}, bf16[256,1536]{1,0:T(8,128)(2,1)}, ...), branch_computations={%region_0.0_spmd, %region_1.0_spmd, %region_2.0_spmd, %region_3.0_... | conditional | flops 228004003840 | bytes 29810188 | solution.py:413
  2.7 0.0 copy-start.6
  2.7 0.0 copy-start.16
  2.7 2.4 %pack.32 = bf16[6,256,128]{2,1,0:T(8,128)(2,1)} custom-call(s32[64]{0:T(128)S(1)} %get-tuple-element.207.schedule, bf16[256,1536]{1,0:T(8,128)(2,1)} %get-tuple-element.196.refs_0_.q), custom_call_target="tpu_custom_call" | custom-call | flops 1000000 | bytes 100000 | tf_op jit(solution)/shard_map/cond/branch_6_fun/pack/pallas_call | solution.py:107
  5.2 0.0 copy-start.26
  5.2 3.2 %collective-permute-start.42 = (bf16[6,256,128]{2,1,0:T(8,128)(2,1)}, bf16[6,256,128]{2,1,0:T(8,128)(2,1)S(1)}, u32[]{:S(2)}, u32[]{:S(2)}) collective-permute-start(bf16[6,256,128]{2,1,0:T(8,128)(2,1)} %pack.32), channel_id=1, source_target_pairs={{0,8},{1,9},{2,10},{3,11},{4,12},{5,13},{6,14},{7,15},{8,0},{9,1},... | collective-permute-start | bytes 1179656 | tf_op jit(solution)/shard_map/cond/branch_6_fun/ppermute | solution.py:369
  8.4 0.0 copy-done.6
  8.4 2.1 %pack.33 = (bf16[2,6,256,128]{3,2,1,0:T(8,128)(2,1)S(1)}, bf16[2,2,256,128]{3,2,1,0:T(8,128)(2,1)S(1)}, bf16[2,3,256,128]{3,2,1,0:T(8,128)(2,1)S(1)}) custom-call(s32[64]{0:T(128)S(1)} %get-tuple-element.207.schedule, bf16[256,1536]{1,0:T(8,128)(2,1)S(1)} %copy-done.6, bf16[256,1536]{1,0:T(8,128)(2,1)} %get-tuple-element.200.refs_1_.v), custom_call_target="tpu_custom_call" | custom-call | flops 1000000 | bytes 100000 | tf_op jit(solution)/shard_map/cond/branch_6_fun/pack/pallas_call | solution.py:107
  10.5 2.9 %collective-permute-start.44 = (bf16[2,6,256,128]{3,2,1,0:T(8,128)(2,1)S(1)}, bf16[2,6,256,128]{3,2,1,0:T(8,128)(2,1)S(1)}, u32[]{:S(2)}, u32[]{:S(2)}) collective-permute-start(bf16[2,6,256,128]{3,2,1,0:T(8,128)(2,1)S(1)} %get-tuple-element.201), channel_id=1, source_target_pairs={{1,0},{2,1},{3,2},{4,3},{5,4},{6,5},{7,6},{9,8},{10,9},{11,10},{12... | collective-permute-start | bytes 2359304 | tf_op jit(solution)/shard_map/cond/branch_6_fun/ppermute | solution.py:369
  13.3 3.0 %collective-permute-start.43 = (bf16[2,6,256,128]{3,2,1,0:T(8,128)(2,1)S(1)}, bf16[2,6,256,128]{3,2,1,0:T(8,128)(2,1)S(1)}, u32[]{:S(2)}, u32[]{:S(2)}) collective-permute-start(bf16[2,6,256,128]{3,2,1,0:T(8,128)(2,1)S(1)} %get-tuple-element.201), channel_id=1, source_target_pairs={{0,1},{1,2},{2,3},{3,4},{4,5},{5,6},{6,7},{8,9},{9,10},{10,11},{11... | collective-permute-start | bytes 2359304 | tf_op jit(solution)/shard_map/cond/branch_6_fun/ppermute | solution.py:369
  16.4 0.0 copy-done.16
  16.4 0.0 copy-done.26
  16.4 1.7 %alone.15.refs_1_ = bf16[256,1536]{1,0:T(8,128)(2,1)} custom-call(s32[64]{0:T(128)S(1)} %get-tuple-element.207.schedule, bf16[256,1536]{1,0:T(8,128)(2,1)S(1)} %copy-done.26, bf16[256,1536]{1,0:T(8,128)(2,1)S(1)} %copy-done.6, bf16[256,1536]{1,0:T(8,128)(2,1)S(1)} %copy-done.16), custom_call_target="tpu_custom_call" | custom-call | flops 20000000000 | bytes 100000 | tf_op jit(solution)/shard_map/cond/branch_6_fun/alone/pallas_call | solution.py:107
  18.1 1.9 %collective-permute-start.47 = (bf16[2,3,256,128]{3,2,1,0:T(8,128)(2,1)S(1)}, bf16[2,3,256,128]{3,2,1,0:T(8,128)(2,1)S(1)}, u32[]{:S(2)}, u32[]{:S(2)}) collective-permute-start(bf16[2,3,256,128]{3,2,1,0:T(8,128)(2,1)S(1)} %get-tuple-element.208), channel_id=1, source_target_pairs={{1,0},{2,1},{3,2},{4,3},{5,4},{6,5},{7,6},{9,8},{10,9},{11,10},{12... | collective-permute-start | bytes 1179656 | tf_op jit(solution)/shard_map/cond/branch_6_fun/ppermute | solution.py:369
  20.0 3.6 %collective-permute-start.46 = (bf16[2,3,256,128]{3,2,1,0:T(8,128)(2,1)S(1)}, bf16[2,3,256,128]{3,2,1,0:T(8,128)(2,1)S(1)}, u32[]{:S(2)}, u32[]{:S(2)}) collective-permute-start(bf16[2,3,256,128]{3,2,1,0:T(8,128)(2,1)S(1)} %get-tuple-element.208), channel_id=1, source_target_pairs={{0,1},{1,2},{2,3},{3,4},{4,5},{5,6},{6,7},{8,9},{9,10},{10,11},{11... | collective-permute-start | bytes 1179656 | tf_op jit(solution)/shard_map/cond/branch_6_fun/ppermute | solution.py:369
  23.7 2.2 %collective-permute-done.42.q = bf16[6,256,128]{2,1,0:T(8,128)(2,1)S(1)} collective-permute-done((bf16[6,256,128]{2,1,0:T(8,128)(2,1)}, bf16[6,256,128]{2,1,0:T(8,128)(2,1)S(1)}, u32[]{:S(2)}, u32[]{:S(2)}) %collective-permute-start.42) | collective-permute-done | bytes 393248 | tf_op jit(solution)/shard_map/cond/branch_6_fun/ppermute | solution.py:369
  25.9 0.0 collective-permute-start.48
  25.9 0.0 collective-permute-done.44.refs_1_
  25.9 3.8 %collective-permute-done.43.refs_0_ = bf16[2,6,256,128]{3,2,1,0:T(8,128)(2,1)S(1)} collective-permute-done((bf16[2,6,256,128]{3,2,1,0:T(8,128)(2,1)S(1)}, bf16[2,6,256,128]{3,2,1,0:T(8,128)(2,1)S(1)}, u32[]{:S(2)}, u32[]{:S(2)}) %collective-permute-start.43) | collective-permute-done | bytes 786464 | tf_op jit(solution)/shard_map/cond/branch_6_fun/ppermute | solution.py:369
  29.7 4.5 %partial_attention.16 = bf16[792,256]{1,0:T(8,128)(2,1)S(1)} custom-call(s32[64]{0:T(128)S(1)} %get-tuple-element.207.schedule, bf16[6,256,128]{2,1,0:T(8,128)(2,1)S(1)} %collective-permute-done.42.q, bf16[256,1536]{1,0:T(8,128)(2,1)S(1)} %copy-done.6, bf16[256,1536]{1,0:T(8,128)(2,1)S(1)} %copy-done.16, ...), custom_call_target="tpu_custom_call" | custom-call | flops 1000000 | bytes 100000 | tf_op jit(solution)/shard_map/cond/branch_6_fun/partial_attention/pallas_call | solution.py:107
  34.2 8.4 %collective-permute-start.45 = (bf16[792,256]{1,0:T(8,128)(2,1)S(1)}, bf16[792,256]{1,0:T(8,128)(2,1)S(1)}, u32[]{:S(2)}, u32[]{:S(2)}) collective-permute-start(bf16[792,256]{1,0:T(8,128)(2,1)S(1)} %partial_attention.16), channel_id=1, source_target_pairs={{8,0},{9,1},{10,2},{11,3},{12,4},{13,5},{14,6},{15,7},{0,8},{1,9},... | collective-permute-start | bytes 1216520 | tf_op jit(solution)/shard_map/cond/branch_6_fun/ppermute | solution.py:369
  42.6 4.6 %local_attention.16 = (f32[6,128,256]{2,1,0:T(8,128)S(1)}, f32[8,256]{1,0:T(8,128)S(1)}) custom-call(s32[64]{0:T(128)S(1)} %get-tuple-element.207.schedule, bf16[256,1536]{1,0:T(8,128)(2,1)S(1)} %copy-done.26, bf16[256,1536]{1,0:T(8,128)(2,1)S(1)} %copy-done.6, bf16[256,1536]{1,0:T(8,128)(2,1)S(1)} %copy-done.16, ...), custom_call_target="tpu_custom_call" | custom-call | flops 1000000 | bytes 100000 | tf_op jit(solution)/shard_map/cond/branch_6_fun/local_attention/pallas_call | solution.py:107
  47.2 0.0 collective-permute-done.48.refs_0_
  47.2 2.5 %timed.15.refs_0_ = bf16[256,1536]{1,0:T(8,128)(2,1)} custom-call(s32[64]{0:T(128)S(1)} %get-tuple-element.207.schedule, bf16[256,1536]{1,0:T(8,128)(2,1)S(1)} %copy-done.26, bf16[256,1536]{1,0:T(8,128)(2,1)S(1)} %copy-done.6, bf16[256,1536]{1,0:T(8,128)(2,1)S(1)} %copy-done.16, ...), custom_call_target="tpu_custom_call", output_to_operand_aliasing={{}: (5, {})} | custom-call | bytes 100000 | tf_op jit(solution)/shard_map/cond/branch_6_fun/timed/pallas_call | solution.py:107
  49.6 0.0 collective-permute-done.47.down
  49.7 0.0 collective-permute-done.46.up
  49.7 3.4 %tall.15.refs_1_ = bf16[256,1536]{1,0:T(8,128)(2,1)} custom-call(s32[64]{0:T(128)S(1)} %get-tuple-element.207.schedule, bf16[256,1536]{1,0:T(8,128)(2,1)S(1)} %copy-done.26, bf16[256,1536]{1,0:T(8,128)(2,1)S(1)} %copy-done.6, bf16[256,1536]{1,0:T(8,128)(2,1)S(1)} %copy-done.16, ...), custom_call_target="tpu_custom_call", output_to_operand_aliasing={{}: (6, {})} | custom-call | flops 99999997952 | bytes 1000000 | tf_op jit(solution)/shard_map/cond/branch_6_fun/tall/pallas_call | solution.py:107
  53.1 4.8 %collective-permute-done.45.refs_0_ = bf16[792,256]{1,0:T(8,128)(2,1)S(1)} collective-permute-done((bf16[792,256]{1,0:T(8,128)(2,1)S(1)}, bf16[792,256]{1,0:T(8,128)(2,1)S(1)}, u32[]{:S(2)}, u32[]{:S(2)}) %collective-permute-start.45) | collective-permute-done | bytes 405536 | tf_op jit(solution)/shard_map/cond/branch_6_fun/ppermute | solution.py:369
  57.9 2.0 %combine.16 = bf16[256,1536]{1,0:T(8,128)(2,1)} custom-call(s32[64]{0:T(128)S(1)} %get-tuple-element.207.schedule, f32[6,128,256]{2,1,0:T(8,128)S(1)} %get-tuple-element.203.mix, f32[8,256]{1,0:T(8,128)S(1)} %get-tuple-element.204.stat, bf16[792,256]{1,0:T(8,128)(2,1)S(1)} %collective-permute-done.45.refs_0_, ...), custom_call_target="tpu_custom_call", output_to_operand_aliasing={{}: (4, {})} | custom-call | flops 99999997952 | bytes 1000000 | tf_op jit(solution)/shard_map/cond/branch_6_fun/combine/pallas_call | solution.py:107
Async XLA Ops:
  2.7 5.7 %copy-start.6 = (bf16[256,1536]{1,0:T(8,128)(2,1)S(1)}, bf16[256,1536]{1,0:T(8,128)(2,1)}, u32[]{:S(2)}) copy-start(bf16[256,1536]{1,0:T(8,128)(2,1)} %get-tuple-element.199.refs_0_.k) | copy-start | bytes 2359300 | tf_op jit(solution)/shard_map/cond
  2.7 13.7 %copy-start.16 = (bf16[256,1536]{1,0:T(8,128)(2,1)S(1)}, bf16[256,1536]{1,0:T(8,128)(2,1)}, u32[]{:S(2)}) copy-start(bf16[256,1536]{1,0:T(8,128)(2,1)} %get-tuple-element.200.refs_1_.v) | copy-start | bytes 2359300 | tf_op jit(solution)/shard_map/cond
  5.2 11.2 %copy-start.26 = (bf16[256,1536]{1,0:T(8,128)(2,1)S(1)}, bf16[256,1536]{1,0:T(8,128)(2,1)}, u32[]{:S(2)}) copy-start(bf16[256,1536]{1,0:T(8,128)(2,1)} %get-tuple-element.196.refs_0_.q) | copy-start | bytes 2359300 | tf_op jit(solution)/shard_map/cond
  5.2 20.7 %collective-permute-start.42 = (bf16[6,256,128]{2,1,0:T(8,128)(2,1)}, bf16[6,256,128]{2,1,0:T(8,128)(2,1)S(1)}, u32[]{:S(2)}, u32[]{:S(2)}) collective-permute-start(bf16[6,256,128]{2,1,0:T(8,128)(2,1)} %pack.32), channel_id=1, source_target_pairs={{0,8},{1,9},{2,10},{3,11},{4,12},{5,13},{6,14},{7,15},{8,0},{9,1},... | collective-permute-start | bytes 1179656 | tf_op jit(solution)/shard_map/cond/branch_6_fun/ppermute | solution.py:369
  10.5 15.4 %collective-permute-start.44 = (bf16[2,6,256,128]{3,2,1,0:T(8,128)(2,1)S(1)}, bf16[2,6,256,128]{3,2,1,0:T(8,128)(2,1)S(1)}, u32[]{:S(2)}, u32[]{:S(2)}) collective-permute-start(bf16[2,6,256,128]{3,2,1,0:T(8,128)(2,1)S(1)} %get-tuple-element.201), channel_id=1, source_target_pairs={{1,0},{2,1},{3,2},{4,3},{5,4},{6,5},{7,6},{9,8},{10,9},{11,10},{12... | collective-permute-start | bytes 2359304 | tf_op jit(solution)/shard_map/cond/branch_6_fun/ppermute | solution.py:369
  13.3 16.4 %collective-permute-start.43 = (bf16[2,6,256,128]{3,2,1,0:T(8,128)(2,1)S(1)}, bf16[2,6,256,128]{3,2,1,0:T(8,128)(2,1)S(1)}, u32[]{:S(2)}, u32[]{:S(2)}) collective-permute-start(bf16[2,6,256,128]{3,2,1,0:T(8,128)(2,1)S(1)} %get-tuple-element.201), channel_id=1, source_target_pairs={{0,1},{1,2},{2,3},{3,4},{4,5},{5,6},{6,7},{8,9},{9,10},{10,11},{11... | collective-permute-start | bytes 2359304 | tf_op jit(solution)/shard_map/cond/branch_6_fun/ppermute | solution.py:369
  18.1 31.5 %collective-permute-start.47 = (bf16[2,3,256,128]{3,2,1,0:T(8,128)(2,1)S(1)}, bf16[2,3,256,128]{3,2,1,0:T(8,128)(2,1)S(1)}, u32[]{:S(2)}, u32[]{:S(2)}) collective-permute-start(bf16[2,3,256,128]{3,2,1,0:T(8,128)(2,1)S(1)} %get-tuple-element.208), channel_id=1, source_target_pairs={{1,0},{2,1},{3,2},{4,3},{5,4},{6,5},{7,6},{9,8},{10,9},{11,10},{12... | collective-permute-start | bytes 1179656 | tf_op jit(solution)/shard_map/cond/branch_6_fun/ppermute | solution.py:369
  20.0 29.6 %collective-permute-start.46 = (bf16[2,3,256,128]{3,2,1,0:T(8,128)(2,1)S(1)}, bf16[2,3,256,128]{3,2,1,0:T(8,128)(2,1)S(1)}, u32[]{:S(2)}, u32[]{:S(2)}) collective-permute-start(bf16[2,3,256,128]{3,2,1,0:T(8,128)(2,1)S(1)} %get-tuple-element.208), channel_id=1, source_target_pairs={{0,1},{1,2},{2,3},{3,4},{4,5},{5,6},{6,7},{8,9},{9,10},{10,11},{11... | collective-permute-start | bytes 1179656 | tf_op jit(solution)/shard_map/cond/branch_6_fun/ppermute | solution.py:369
  25.9 21.3 %collective-permute-start.48 = (bf16[2,2,256,128]{3,2,1,0:T(8,128)(2,1)S(1)}, bf16[2,2,256,128]{3,2,1,0:T(8,128)(2,1)S(1)}, u32[]{:S(2)}, u32[]{:S(2)}) collective-permute-start(bf16[2,2,256,128]{3,2,1,0:T(8,128)(2,1)S(1)} %get-tuple-element.210), channel_id=1, source_target_pairs={{0,8},{1,9},{2,10},{3,11},{4,12},{5,13},{6,14},{7,15},{8,0},{9,1},... | collective-permute-start | bytes 786440 | tf_op jit(solution)/shard_map/cond/branch_6_fun/ppermute | solution.py:369
  34.2 23.7 %collective-permute-start.45 = (bf16[792,256]{1,0:T(8,128)(2,1)S(1)}, bf16[792,256]{1,0:T(8,128)(2,1)S(1)}, u32[]{:S(2)}, u32[]{:S(2)}) collective-permute-start(bf16[792,256]{1,0:T(8,128)(2,1)S(1)} %partial_attention.16), channel_id=1, source_target_pairs={{8,0},{9,1},{10,2},{11,3},{12,4},{13,5},{14,6},{15,7},{0,8},{1,9},... | collective-permute-start | bytes 1216520 | tf_op jit(solution)/shard_map/cond/branch_6_fun/ppermute | solution.py:369
where the time goes:
time: 60.4 us; the launch traced here: 60.1 us
  Pallas kernels  25 us (41%)
  starting transfers between devices  23.1 us (38%)
  waiting for transfers between devices  10.8 us (18%)
  between operations  0.8 us (1%)
    pallas_call x8, Pallas kernels, call(): pl.pallas_call(kernel, out_shape=outs, grid_spec=pltpu.PrefetchScalarGrid...  23.2 us
    ppermute x7, starting transfers between devices, move(): return lax.ppermute(value, 'context', pairs)  23.1 us
    ppermute x7, waiting for transfers between devices, move(): return lax.ppermute(value, 'context', pairs)  10.8 us
    pallas_call x1, Pallas kernels, plan(): pl.pallas_call(functools.partial(plan_kernel, time_tiles), out_shape=[jax...  1.8 us
  transfers between devices with their start and end apart: 7, of which 3 were waited for; matrix products, arithmetic and copies ran while one was open for 0% of the time, Pallas kernels for 31%

commit v1 on v0

--- a/solution.py
+++ b/solution.py
@@ -15,7 +15,7 @@
 MASKED = -1e30
 SCALE2 = math.log2(math.e) / math.sqrt(HD)
 PACK_LIMIT = 62
-FILL_EARLY, FILL, WAIT = 2e10, 8e9, 8e9
+FILL_EARLY, FILL, WAIT = 2e10, 1e9, 8e9
 MENU = ((2, 2, 3), (3, 2, 3), (3, 2, 4), (4, 2, 3), (4, 2, 4), (5, 2, 4), (6, 2, 3), (7, 2, 2), (9, 1, 1), (12, 0, 0))
 
 TALL, WIDE, TIMED, UP_OK, DOWN_OK, SIDE_OK = 12, 24, 36, 48, 49, 50
@@ -389,7 +389,7 @@
         others = [move(across, pairs) for pairs in routes]
     parts = [partial_attention(ready, query, k, v, near) for query in sent]
     if c:
-        later = after(later, *(sent if a == 5 else []), *([out] if d else sent))
+        later = after(later, *(sent if a < 6 and a != 4 else []), *([out] if d and early else sent))
         heights = [move(later, upward), move(later, downward)]
     mix, stat = local_attention(after(schedule, *parts), q, k, v, near, a)
     parts = [move(part, back) for part, back in zip(parts, backs)]

time: 60.4 us -> 47.6 us (0.79)
  starting transfers between devices: 23.1 us -> 14.9 us
  waiting for transfers between devices: 10.8 us -> 8.19 us
  Pallas kernels: 25 us -> 22.8 us
    ppermute x7, starting transfers between devices: 23.1 us -> 14.9 us  [move(): return lax.ppermute(value, 'context', pairs)]
    ppermute x7, waiting for transfers between devices: 10.8 us -> 8.19 us  [move(): return lax.ppermute(value, 'context', pairs)]
    pallas_call x8, Pallas kernels: 23.2 us -> 21 us  [call(): pl.pallas_call(kernel, out_shape=outs, grid_spec=pltpu.PrefetchScalarGrid...]
  transfers between devices with their start and end apart: 7 -> 7, of which waited for: 3 -> 2; matrix products, arithmetic and copies ran while one was open for 0% -> 0% of each run, Pallas kernels for 31% -> 36%
where the time goes in v1:
time: 47.6 us; the launch traced here: 47.3 us
  Pallas kernels  22.8 us (48%)
  starting transfers between devices  14.9 us (31%)
  waiting for transfers between devices  8.19 us (17%)
  between operations  0.8 us (2%)
  loops' own time  0.63 us (1%)
    pallas_call x8, Pallas kernels, call(): pl.pallas_call(kernel, out_shape=outs, grid_spec=pltpu.PrefetchScalarGrid...  21 us
    ppermute x7, starting transfers between devices, move(): return lax.ppermute(value, 'context', pairs)  14.9 us
    ppermute x7, waiting for transfers between devices, move(): return lax.ppermute(value, 'context', pairs)  8.19 us
    pallas_call x1, Pallas kernels, plan(): pl.pallas_call(functools.partial(plan_kernel, time_tiles), out_shape=[jax...  1.8 us
  transfers between devices with their start and end apart: 7, of which 2 were waited for; matrix products, arithmetic and copies ran while one was open for 0% of the time, Pallas kernels for 36%

profile of v1, /device:TPU:1, one launch (start us, length us, event | category | flops | bytes accessed | tf_op | source)
XLA Modules:
  0.0 47.3 jit_solution(6737044710995948802)
XLA Ops:
  0.0 1.8 %plan.1 = (s32[64]{0:T(128)S(1)}, s32[1]{0:T(128)}) custom-call(s32[3,12]{1,0:T(4,128)} %bitcast.3, s32[1]{0:T(128)} %bitcast.1.index), custom_call_target="tpu_custom_call" | custom-call | tf_op jit(solution)/shard_map/plan/pallas_call | solution.py:78
  2.4 44.7 %conditional.1 = (bf16[256,1536]{1,0:T(8,128)(2,1)}) conditional(s32[]{:T(128)} %bitcast.2, (s32[64]{0:T(128)S(1)}, bf16[256,1536]{1,0:T(8,128)(2,1)}, bf16[256,1536]{1,0:T(8,128)(2,1)}, bf16[256,1536]{1,0:T(8,128)(2,1)}) %tuple.94, (s32[64]{0:T(128)S(1)}, bf16[256,1536]{1,0:T(8,128)(2,1)}, ...), branch_computations={%region_0.0_spmd, %region_1.0_spmd, %region_2.0_spmd, %region_3.0_... | conditional | flops 228004003840 | bytes 29810188 | solution.py:413
  2.5 0.0 copy-start.3
  2.5 0.0 copy-start.13
  2.5 2.3 %pack.26 = bf16[4,256,128]{2,1,0:T(8,128)(2,1)} custom-call(s32[64]{0:T(128)S(1)} %get-tuple-element.159.schedule, bf16[256,1536]{1,0:T(8,128)(2,1)} %get-tuple-element.148.refs_0_.q), custom_call_target="tpu_custom_call" | custom-call | flops 1000000 | bytes 100000 | tf_op jit(solution)/shard_map/cond/branch_3_fun/pack/pallas_call | solution.py:107
  4.8 0.0 copy-start.23
  4.8 3.2 %collective-permute-start.21 = (bf16[4,256,128]{2,1,0:T(8,128)(2,1)}, bf16[4,256,128]{2,1,0:T(8,128)(2,1)S(1)}, u32[]{:S(2)}, u32[]{:S(2)}) collective-permute-start(bf16[4,256,128]{2,1,0:T(8,128)(2,1)} %pack.26), channel_id=1, source_target_pairs={{0,8},{1,9},{2,10},{3,11},{4,12},{5,13},{6,14},{7,15},{8,0},{9,1},... | collective-permute-start | bytes 786440 | tf_op jit(solution)/shard_map/cond/branch_3_fun/ppermute | solution.py:369
  8.0 0.0 copy-done.3
  8.0 2.0 %pack.27 = (bf16[2,4,256,128]{3,2,1,0:T(8,128)(2,1)S(1)}, bf16[2,2,256,128]{3,2,1,0:T(8,128)(2,1)S(1)}, bf16[2,3,256,128]{3,2,1,0:T(8,128)(2,1)S(1)}) custom-call(s32[64]{0:T(128)S(1)} %get-tuple-element.159.schedule, bf16[256,1536]{1,0:T(8,128)(2,1)S(1)} %copy-done.3, bf16[256,1536]{1,0:T(8,128)(2,1)} %get-tuple-element.152.refs_1_.v), custom_call_target="tpu_custom_call" | custom-call | flops 1000000 | bytes 100000 | tf_op jit(solution)/shard_map/cond/branch_3_fun/pack/pallas_call | solution.py:107
  10.0 2.9 %collective-permute-start.23 = (bf16[2,4,256,128]{3,2,1,0:T(8,128)(2,1)S(1)}, bf16[2,4,256,128]{3,2,1,0:T(8,128)(2,1)S(1)}, u32[]{:S(2)}, u32[]{:S(2)}) collective-permute-start(bf16[2,4,256,128]{3,2,1,0:T(8,128)(2,1)S(1)} %get-tuple-element.153), channel_id=1, source_target_pairs={{1,0},{2,1},{3,2},{4,3},{5,4},{6,5},{7,6},{9,8},{10,9},{11,10},{12... | collective-permute-start | bytes 1572872 | tf_op jit(solution)/shard_map/cond/branch_3_fun/ppermute | solution.py:369
  12.9 3.0 %collective-permute-start.22 = (bf16[2,4,256,128]{3,2,1,0:T(8,128)(2,1)S(1)}, bf16[2,4,256,128]{3,2,1,0:T(8,128)(2,1)S(1)}, u32[]{:S(2)}, u32[]{:S(2)}) collective-permute-start(bf16[2,4,256,128]{3,2,1,0:T(8,128)(2,1)S(1)} %get-tuple-element.153), channel_id=1, source_target_pairs={{0,1},{1,2},{2,3},{3,4},{4,5},{5,6},{6,7},{8,9},{9,10},{10,11},{11... | collective-permute-start | bytes 1572872 | tf_op jit(solution)/shard_map/cond/branch_3_fun/ppermute | solution.py:369
  15.9 0.0 copy-done.13
  15.9 0.0 copy-done.23
  16.0 2.7 %alone.12.refs_1_ = bf16[256,1536]{1,0:T(8,128)(2,1)} custom-call(s32[64]{0:T(128)S(1)} %get-tuple-element.159.schedule, bf16[256,1536]{1,0:T(8,128)(2,1)S(1)} %copy-done.23, bf16[256,1536]{1,0:T(8,128)(2,1)S(1)} %copy-done.3, bf16[256,1536]{1,0:T(8,128)(2,1)S(1)} %copy-done.13), custom_call_target="tpu_custom_call" | custom-call | flops 20000000000 | bytes 100000 | tf_op jit(solution)/shard_map/cond/branch_3_fun/alone/pallas_call | solution.py:107
  18.7 0.1 collective-permute-start.27
  18.8 1.9 %collective-permute-start.26 = (bf16[2,3,256,128]{3,2,1,0:T(8,128)(2,1)S(1)}, bf16[2,3,256,128]{3,2,1,0:T(8,128)(2,1)S(1)}, u32[]{:S(2)}, u32[]{:S(2)}) collective-permute-start(bf16[2,3,256,128]{3,2,1,0:T(8,128)(2,1)S(1)} %get-tuple-element.160), channel_id=1, source_target_pairs={{1,0},{2,1},{3,2},{4,3},{5,4},{6,5},{7,6},{9,8},{10,9},{11,10},{12... | collective-permute-start | bytes 1179656 | tf_op jit(solution)/shard_map/cond/branch_3_fun/ppermute | solution.py:369
  20.7 0.0 collective-permute-done.21.q
  20.7 3.6 %collective-permute-start.25 = (bf16[2,3,256,128]{3,2,1,0:T(8,128)(2,1)S(1)}, bf16[2,3,256,128]{3,2,1,0:T(8,128)(2,1)S(1)}, u32[]{:S(2)}, u32[]{:S(2)}) collective-permute-start(bf16[2,3,256,128]{3,2,1,0:T(8,128)(2,1)S(1)} %get-tuple-element.160), channel_id=1, source_target_pairs={{0,1},{1,2},{2,3},{3,4},{4,5},{5,6},{6,7},{8,9},{9,10},{10,11},{11... | collective-permute-start | bytes 1179656 | tf_op jit(solution)/shard_map/cond/branch_3_fun/ppermute | solution.py:369
  24.4 0.0 collective-permute-done.23.refs_1_
  24.4 4.7 %collective-permute-done.22.refs_0_ = bf16[2,4,256,128]{3,2,1,0:T(8,128)(2,1)S(1)} collective-permute-done((bf16[2,4,256,128]{3,2,1,0:T(8,128)(2,1)S(1)}, bf16[2,4,256,128]{3,2,1,0:T(8,128)(2,1)S(1)}, u32[]{:S(2)}, u32[]{:S(2)}) %collective-permute-start.22) | collective-permute-done | bytes 524320 | tf_op jit(solution)/shard_map/cond/branch_3_fun/ppermute | solution.py:369
  29.1 3.2 %partial_attention.13 = bf16[536,256]{1,0:T(8,128)(2,1)S(1)} custom-call(s32[64]{0:T(128)S(1)} %get-tuple-element.159.schedule, bf16[4,256,128]{2,1,0:T(8,128)(2,1)S(1)} %collective-permute-done.21.q, bf16[256,1536]{1,0:T(8,128)(2,1)S(1)} %copy-done.3, bf16[256,1536]{1,0:T(8,128)(2,1)S(1)} %copy-done.13, ...), custom_call_target="tpu_custom_call" | custom-call | flops 1000000 | bytes 100000 | tf_op jit(solution)/shard_map/cond/branch_3_fun/partial_attention/pallas_call | solution.py:107
  32.3 0.1 collective-permute-start.24
  32.4 3.2 %local_attention.13 = (f32[4,128,256]{2,1,0:T(8,128)S(1)}, f32[8,256]{1,0:T(8,128)S(1)}) custom-call(s32[64]{0:T(128)S(1)} %get-tuple-element.159.schedule, bf16[256,1536]{1,0:T(8,128)(2,1)S(1)} %copy-done.23, bf16[256,1536]{1,0:T(8,128)(2,1)S(1)} %copy-done.3, bf16[256,1536]{1,0:T(8,128)(2,1)S(1)} %copy-done.13, ...), custom_call_target="tpu_custom_call" | custom-call | flops 1000000 | bytes 100000 | tf_op jit(solution)/shard_map/cond/branch_3_fun/local_attention/pallas_call | solution.py:107
  35.6 0.0 collective-permute-done.27.refs_0_
  35.7 2.5 %timed.12.refs_0_ = bf16[256,1536]{1,0:T(8,128)(2,1)} custom-call(s32[64]{0:T(128)S(1)} %get-tuple-element.159.schedule, bf16[256,1536]{1,0:T(8,128)(2,1)S(1)} %copy-done.23, bf16[256,1536]{1,0:T(8,128)(2,1)S(1)} %copy-done.3, bf16[256,1536]{1,0:T(8,128)(2,1)S(1)} %copy-done.13, ...), custom_call_target="tpu_custom_call", output_to_operand_aliasing={{}: (5, {})} | custom-call | flops 8000000000 | bytes 100000 | tf_op jit(solution)/shard_map/cond/branch_3_fun/timed/pallas_call | solution.py:107
  38.1 0.0 collective-permute-done.26.down
  38.1 0.0 collective-permute-done.25.up
  38.1 3.4 %tall.12.refs_1_ = bf16[256,1536]{1,0:T(8,128)(2,1)} custom-call(s32[64]{0:T(128)S(1)} %get-tuple-element.159.schedule, bf16[256,1536]{1,0:T(8,128)(2,1)S(1)} %copy-done.23, bf16[256,1536]{1,0:T(8,128)(2,1)S(1)} %copy-done.3, bf16[256,1536]{1,0:T(8,128)(2,1)S(1)} %copy-done.13, ...), custom_call_target="tpu_custom_call", output_to_operand_aliasing={{}: (6, {})} | custom-call | flops 99999997952 | bytes 1000000 | tf_op jit(solution)/shard_map/cond/branch_3_fun/tall/pallas_call | solution.py:107
  41.6 3.4 %collective-permute-done.24.refs_0_ = bf16[536,256]{1,0:T(8,128)(2,1)S(1)} collective-permute-done((bf16[536,256]{1,0:T(8,128)(2,1)S(1)}, bf16[536,256]{1,0:T(8,128)(2,1)S(1)}, u32[]{:S(2)}, u32[]{:S(2)}) %collective-permute-start.24) | collective-permute-done | bytes 274464 | tf_op jit(solution)/shard_map/cond/branch_3_fun/ppermute | solution.py:369
  45.0 1.7 %combine.13 = bf16[256,1536]{1,0:T(8,128)(2,1)} custom-call(s32[64]{0:T(128)S(1)} %get-tuple-element.159.schedule, f32[4,128,256]{2,1,0:T(8,128)S(1)} %get-tuple-element.155.mix, f32[8,256]{1,0:T(8,128)S(1)} %get-tuple-element.156.stat, bf16[536,256]{1,0:T(8,128)(2,1)S(1)} %collective-permute-done.24.refs_0_, ...), custom_call_target="tpu_custom_call", output_to_operand_aliasing={{}: (4, {})} | custom-call | flops 99999997952 | bytes 1000000 | tf_op jit(solution)/shard_map/cond/branch_3_fun/combine/pallas_call | solution.py:107
Async XLA Ops:
  2.5 5.6 %copy-start.3 = (bf16[256,1536]{1,0:T(8,128)(2,1)S(1)}, bf16[256,1536]{1,0:T(8,128)(2,1)}, u32[]{:S(2)}) copy-start(bf16[256,1536]{1,0:T(8,128)(2,1)} %get-tuple-element.151.refs_0_.k) | copy-start | bytes 2359300 | tf_op jit(solution)/shard_map/cond
  2.5 13.5 %copy-start.13 = (bf16[256,1536]{1,0:T(8,128)(2,1)S(1)}, bf16[256,1536]{1,0:T(8,128)(2,1)}, u32[]{:S(2)}) copy-start(bf16[256,1536]{1,0:T(8,128)(2,1)} %get-tuple-element.152.refs_1_.v) | copy-start | bytes 2359300 | tf_op jit(solution)/shard_map/cond
  4.8 11.2 %copy-start.23 = (bf16[256,1536]{1,0:T(8,128)(2,1)S(1)}, bf16[256,1536]{1,0:T(8,128)(2,1)}, u32[]{:S(2)}) copy-start(bf16[256,1536]{1,0:T(8,128)(2,1)} %get-tuple-element.148.refs_0_.q) | copy-start | bytes 2359300 | tf_op jit(solution)/shard_map/cond
  4.8 15.9 %collective-permute-start.21 = (bf16[4,256,128]{2,1,0:T(8,128)(2,1)}, bf16[4,256,128]{2,1,0:T(8,128)(2,1)S(1)}, u32[]{:S(2)}, u32[]{:S(2)}) collective-permute-start(bf16[4,256,128]{2,1,0:T(8,128)(2,1)} %pack.26), channel_id=1, source_target_pairs={{0,8},{1,9},{2,10},{3,11},{4,12},{5,13},{6,14},{7,15},{8,0},{9,1},... | collective-permute-start | bytes 786440 | tf_op jit(solution)/shard_map/cond/branch_3_fun/ppermute | solution.py:369
  10.0 14.4 %collective-permute-start.23 = (bf16[2,4,256,128]{3,2,1,0:T(8,128)(2,1)S(1)}, bf16[2,4,256,128]{3,2,1,0:T(8,128)(2,1)S(1)}, u32[]{:S(2)}, u32[]{:S(2)}) collective-permute-start(bf16[2,4,256,128]{3,2,1,0:T(8,128)(2,1)S(1)} %get-tuple-element.153), channel_id=1, source_target_pairs={{1,0},{2,1},{3,2},{4,3},{5,4},{6,5},{7,6},{9,8},{10,9},{11,10},{12... | collective-permute-start | bytes 1572872 | tf_op jit(solution)/shard_map/cond/branch_3_fun/ppermute | solution.py:369
  12.9 16.2 %collective-permute-start.22 = (bf16[2,4,256,128]{3,2,1,0:T(8,128)(2,1)S(1)}, bf16[2,4,256,128]{3,2,1,0:T(8,128)(2,1)S(1)}, u32[]{:S(2)}, u32[]{:S(2)}) collective-permute-start(bf16[2,4,256,128]{3,2,1,0:T(8,128)(2,1)S(1)} %get-tuple-element.153), channel_id=1, source_target_pairs={{0,1},{1,2},{2,3},{3,4},{4,5},{5,6},{6,7},{8,9},{9,10},{10,11},{11... | collective-permute-start | bytes 1572872 | tf_op jit(solution)/shard_map/cond/branch_3_fun/ppermute | solution.py:369
  18.7 17.0 %collective-permute-start.27 = (bf16[2,2,256,128]{3,2,1,0:T(8,128)(2,1)S(1)}, bf16[2,2,256,128]{3,2,1,0:T(8,128)(2,1)S(1)}, u32[]{:S(2)}, u32[]{:S(2)}) collective-permute-start(bf16[2,2,256,128]{3,2,1,0:T(8,128)(2,1)S(1)} %get-tuple-element.162), channel_id=1, source_target_pairs={{0,8},{1,9},{2,10},{3,11},{4,12},{5,13},{6,14},{7,15},{8,0},{9,1},... | collective-permute-start | bytes 786440 | tf_op jit(solution)/shard_map/cond/branch_3_fun/ppermute | solution.py:369
  18.8 19.3 %collective-permute-start.26 = (bf16[2,3,256,128]{3,2,1,0:T(8,128)(2,1)S(1)}, bf16[2,3,256,128]{3,2,1,0:T(8,128)(2,1)S(1)}, u32[]{:S(2)}, u32[]{:S(2)}) collective-permute-start(bf16[2,3,256,128]{3,2,1,0:T(8,128)(2,1)S(1)} %get-tuple-element.160), channel_id=1, source_target_pairs={{1,0},{2,1},{3,2},{4,3},{5,4},{6,5},{7,6},{9,8},{10,9},{11,10},{12... | collective-permute-start | bytes 1179656 | tf_op jit(solution)/shard_map/cond/branch_3_fun/ppermute | solution.py:369
  20.7 17.4 %collective-permute-start.25 = (bf16[2,3,256,128]{3,2,1,0:T(8,128)(2,1)S(1)}, bf16[2,3,256,128]{3,2,1,0:T(8,128)(2,1)S(1)}, u32[]{:S(2)}, u32[]{:S(2)}) collective-permute-start(bf16[2,3,256,128]{3,2,1,0:T(8,128)(2,1)S(1)} %get-tuple-element.160), channel_id=1, source_target_pairs={{0,1},{1,2},{2,3},{3,4},{4,5},{5,6},{6,7},{8,9},{9,10},{10,11},{11... | collective-permute-start | bytes 1179656 | tf_op jit(solution)/shard_map/cond/branch_3_fun/ppermute | solution.py:369
  32.3 12.7 %collective-permute-start.24 = (bf16[536,256]{1,0:T(8,128)(2,1)S(1)}, bf16[536,256]{1,0:T(8,128)(2,1)S(1)}, u32[]{:S(2)}, u32[]{:S(2)}) collective-permute-start(bf16[536,256]{1,0:T(8,128)(2,1)S(1)} %partial_attention.13), channel_id=1, source_target_pairs={{8,0},{9,1},{10,2},{11,3},{12,4},{13,5},{14,6},{15,7},{0,8},{1,9},... | collective-permute-start | bytes 823304 | tf_op jit(solution)/shard_map/cond/branch_3_fun/ppermute | solution.py:369
